TPU v7x, 32 devices: a whole 2x2x4 slice. The times are simulated.
32 devices in a mesh: dp: 8 (over z, core), fsdp: 4 (over y, x).
Axes of the slice: x: 2, y: 2, z: 4, core: 2. Of those that a mesh axis runs over, the one named last changes fastest.
Arguments:
- pixels: bfloat16 [32768, 768], P(('dp', 'fsdp')), may hold values from -6 to 6
- valid_mask: int32 [32768, 768], P(('dp', 'fsdp')), may hold values from 0 to 1
- size_groups: int32 [32], P(('dp', 'fsdp')), may hold values from 0 to 2
- code_index: int32 [4, 8192], P(None, ('dp', 'fsdp')), may hold values from 0 to 16383, as said below
- w_pixel: float32 [2, 768, 512], P(None, 'fsdp', 'dp'), may hold values from -0.625 to 0.625
- w_res: float32 [4, 4608, 512], P(None, 'fsdp', 'dp'), may hold values from -0.1875 to 0.1875
- w_scale: float32 [2, 2048, 512], P(None, 'fsdp', 'dp'), may hold values from -0.5 to 0.5
- w_latent: float32 [2, 512, 256], P(None, 'fsdp', 'dp'), may hold values from -0.75 to 0.75
- norm_gains: float32 [8, 512], replicated, may hold values from -0.9 to 1.5
- moment_pixel: float32 [2, 768, 512], P(None, 'fsdp', 'dp'), may hold values from -4.4703484e-08 to 4.4703484e-08
- moment_res: float32 [4, 4608, 512], P(None, 'fsdp', 'dp'), may hold values from -4.4703484e-08 to 4.4703484e-08
- moment_scale: float32 [2, 2048, 512], P(None, 'fsdp', 'dp'), may hold values from -4.4703484e-08 to 4.4703484e-08
- moment_latent: float32 [2, 512, 256], P(None, 'fsdp', 'dp'), may hold values from -4.4703484e-08 to 4.4703484e-08
- moment_gains: float32 [8, 512], replicated, may hold values from -1.4901161e-07 to 1.4901161e-07
- second_pixel: float32 [2, 768, 512], P(None, 'fsdp', 'dp'), may hold values from 7.84e-18 to 3.136e-17
- second_res: float32 [4, 4608, 512], P(None, 'fsdp', 'dp'), may hold values from 7.84e-18 to 3.136e-17
- second_scale: float32 [2, 2048, 512], P(None, 'fsdp', 'dp'), may hold values from 7.84e-18 to 3.136e-17
- second_latent: float32 [2, 512, 256], P(None, 'fsdp', 'dp'), may hold values from 7.84e-18 to 3.136e-17
- second_gains: float32 [8, 512], replicated, may hold values from 1e-16 to 4e-16
- ema_counts: float32 [16384], P(('dp', 'fsdp')), may hold values from 0.5 to 4
- ema_sums: float32 [16384, 256], P(('dp', 'fsdp')), may hold values from -6 to 6
Outputs:
- loss_parts: float32 [3], replicated
- grad_norm: float32 [1], replicated
- next_pixel: float32 [2, 768, 512], P(None, 'fsdp', 'dp')
- next_moment_pixel: float32 [2, 768, 512], P(None, 'fsdp', 'dp')
- next_second_pixel: float32 [2, 768, 512], P(None, 'fsdp', 'dp')
- copy_pixel: bfloat16 [2, 768, 512], P(None, 'fsdp', 'dp')
- next_res: float32 [4, 4608, 512], P(None, 'fsdp', 'dp')
- next_moment_res: float32 [4, 4608, 512], P(None, 'fsdp', 'dp')
- next_second_res: float32 [4, 4608, 512], P(None, 'fsdp', 'dp')
- copy_res: bfloat16 [4, 4608, 512], P(None, 'fsdp', 'dp')
- next_scale: float32 [2, 2048, 512], P(None, 'fsdp', 'dp')
- next_moment_scale: float32 [2, 2048, 512], P(None, 'fsdp', 'dp')
- next_second_scale: float32 [2, 2048, 512], P(None, 'fsdp', 'dp')
- copy_scale: bfloat16 [2, 2048, 512], P(None, 'fsdp', 'dp')
- next_latent: float32 [2, 512, 256], P(None, 'fsdp', 'dp')
- next_moment_latent: float32 [2, 512, 256], P(None, 'fsdp', 'dp')
- next_second_latent: float32 [2, 512, 256], P(None, 'fsdp', 'dp')
- copy_latent: bfloat16 [2, 512, 256], P(None, 'fsdp', 'dp')
- next_gains: float32 [8, 512], replicated
- next_moment_gains: float32 [8, 512], replicated
- next_second_gains: float32 [8, 512], replicated
- next_counts: float32 [16384], P(('dp', 'fsdp'))
- next_sums: float32 [16384, 256], P(('dp', 'fsdp'))
- codebook: float32 [16384, 256], P(('dp', 'fsdp'))
- codebook_copy: bfloat16 [16384, 256], P(('dp', 'fsdp'))
Inputs may be any that keep to these rules, and one draw needn't show every extreme that they name: `code_index`: among the 4 x 256 codes of one device's positions, at most 64 lie in any one device's block of 16384 / 32 consecutive codes, and on every device some block holds exactly 64 of them.
All inputs are finite; a program needn't handle non-finite values.
Results may differ from a plain program's by a relative error of at most 0.0061.
Values may be sent and summed in bfloat16 or wider, within the bound.
No kernel may reach another device: no remote copies, remote signals or barrier semaphores. Data moves between devices by JAX's collectives and lax.ppermute only.
A program may use at most 256 MiB of HBM per device.

v0:
```python
import jax
import jax.numpy as jnp
from jax import lax
from jax.sharding import PartitionSpec as P

C = 512
ZD = 256
K = 16384
GROUPS = 32
SIDE = 32
DEPTH = 4
STEP = 5
HIGH = lax.Precision.HIGHEST
TAPS = [(dy, dx) for dy in (-1, 0, 1) for dx in (-1, 0, 1)]
COMMIT_WEIGHT = 0.25
CLIP_AT = 1e-05
EMA_DECAY = 0.8
WEIGHT_RATE = 0.03
GAIN_RATE = 0.4


def geometry(groups, size, width):
    span = jnp.left_shift(jnp.ones_like(groups), groups)
    sides = size // 4 * span
    tile = jnp.arange(16, dtype=jnp.int32)[None, :]
    image = tile // 4 // span[:, None] * (4 // span[:, None]) + tile % 4 // span[:, None]
    member = (image[:, :, None] == jnp.arange(16, dtype=jnp.int32)[None, None, :]).astype(
        jnp.float32
    )
    count = (sides * sides).astype(jnp.float32) * (width // GROUPS)
    return (sides, member, count)


def image_means(field, member, count):
    batch, size, _, width = field.shape
    tile = size // 4
    sums = jnp.sum(field.reshape(batch, 4, tile, 4, tile, width), axis=(2, 4)).reshape(
        batch, 16, width
    )
    per_image = jnp.einsum("btm,btc->bmc", member, sums, precision=HIGH)
    grouped = (
        jnp.sum(per_image.reshape(batch, 16, GROUPS, width // GROUPS), axis=3)
        / count[:, None, None]
    )
    spread = jnp.einsum("btm,bmg->btg", member, grouped, precision=HIGH)
    full = jnp.repeat(spread, width // GROUPS, axis=2).reshape(batch, 4, 1, 4, 1, width)
    return jnp.broadcast_to(full, (batch, 4, tile, 4, tile, width)).reshape(
        batch, size, size, width
    )


def gn_silu(field, gamma, beta, geom):
    mean = image_means(field, geom[1], geom[2])
    centered = field - mean
    var = image_means(centered * centered, geom[1], geom[2])
    return jax.nn.silu(centered * lax.rsqrt(var + 1e-05) * gamma + beta)


def silu_slope(value):
    gate = jax.nn.sigmoid(value)
    return gate * (1.0 + value * (1.0 - gate))


def side_masks(sides, size, delta):
    pos = jnp.arange(size, dtype=jnp.int32)
    near = pos + delta
    inside = (near >= 0) & (near < size)
    same = near[None, :] // sides[:, None] == pos[None, :] // sides[:, None]
    return (inside[None, :] & same).astype(jnp.float32)


def shifted(act, sides, dy, dx):
    size = act.shape[1]
    padded = jnp.pad(act, ((0, 0), (1, 1), (1, 1), (0, 0)))
    part = padded[:, 1 + dy : 1 + dy + size, 1 + dx : 1 + dx + size, :]
    keep = side_masks(sides, size, dy)[:, :, None] * side_masks(sides, size, dx)[:, None, :]
    return part * keep[..., None].astype(act.dtype)


def along_rows(left, right):
    return lax.dot_general(
        left, right, (((0,), (0,)), ((), ())), preferred_element_type=jnp.float32
    )


def along_cols(left, right):
    return lax.dot_general(
        left, right, (((1,), (1,)), ((), ())), preferred_element_type=jnp.float32
    )


def conv_forward(act, taps, geom):
    width = act.shape[3]
    total = jnp.zeros((act.shape[0] * act.shape[1] * act.shape[2], width), jnp.float32)
    for index, (dy, dx) in enumerate(TAPS):
        piece = shifted(act, geom[0], dy, dx).reshape(-1, width)
        total = total + jnp.dot(piece, taps[index], preferred_element_type=jnp.float32)
    return total.reshape(act.shape)


def conv_backward(act, taps, grad_out, geom):
    width = act.shape[3]
    grad_low = grad_out.reshape(-1, width).astype(jnp.bfloat16)
    weight_parts = []
    grad_act = jnp.zeros(act.shape, jnp.float32)
    for index, (dy, dx) in enumerate(TAPS):
        piece = shifted(act, geom[0], dy, dx).reshape(-1, width)
        weight_parts.append(along_rows(piece, grad_low))
        back = along_cols(grad_low, taps[index]).reshape(act.shape)
        grad_act = grad_act + shifted(back, geom[0], -dy, -dx)
    return (jnp.concatenate(weight_parts, axis=0), grad_act)


def block_forward(field, taps_pair, gains, first, geom):
    a_one = gn_silu(field, gains[first], gains[4 + first], geom).astype(jnp.bfloat16)
    t_one = conv_forward(a_one, taps_pair[0], geom)
    a_two = gn_silu(t_one, gains[first + 1], gains[5 + first], geom).astype(jnp.bfloat16)
    t_two = conv_forward(a_two, taps_pair[1], geom)
    return (field + t_two, (field, a_one, t_one, a_two))


def block_backward(grad, kept, taps_pair, gains, first, geom):
    field, a_one, t_one, a_two = kept
    grad_two, d_a_two = conv_backward(a_two, taps_pair[1], grad, geom)
    _, pull = jax.vjp(
        lambda x, g, b: gn_silu(x, g, b, geom), t_one, gains[first + 1], gains[5 + first]
    )
    d_t_one, scale_two, shift_two = pull(d_a_two)
    grad_one, d_a_one = conv_backward(a_one, taps_pair[0], d_t_one, geom)
    _, pull = jax.vjp(lambda x, g, b: gn_silu(x, g, b, geom), field, gains[first], gains[4 + first])
    d_field, scale_one, shift_one = pull(d_a_one)
    return (grad + d_field, (grad_one, grad_two), (scale_one, scale_two, shift_one, shift_two))


def to_depth(field):
    batch, size, _, width = field.shape
    half = size // 2
    parts = field.reshape(batch, half, 2, half, 2, width).transpose(0, 1, 3, 2, 4, 5)
    return parts.reshape(batch * half * half, 4 * width)


def from_depth(rows, batch, size):
    half = size // 2
    width = rows.shape[1] // 4
    parts = rows.reshape(batch, half, half, 2, 2, width).transpose(0, 1, 3, 2, 4, 5)
    return parts.reshape(batch, size, size, width)


def fetch(shard):
    cols = lax.all_gather(shard.astype(jnp.bfloat16), "dp", axis=1, tiled=True)
    return lax.all_gather(cols, "fsdp", axis=0, tiled=True)


def backward_copy(shard, ready):
    return fetch(shard).reshape(ready.shape)


def reduce_grad(full):
    rows = lax.psum_scatter(full, "fsdp", scatter_dimension=0, tiled=True)
    return lax.psum_scatter(rows, "dp", scatter_dimension=1, tiled=True)


def adam_step(weight, moment, second, grad, rate):
    moment_new = 0.5 * moment + 0.5 * grad
    second_new = 0.5 * second + 0.5 * grad * grad
    fix = 1.0 - 0.5**STEP
    weight_new = weight - rate * (
        moment_new / fix / (jnp.sqrt(second_new / fix) + 1e-12) + 0.01 * weight
    )
    return (weight_new, moment_new, second_new)


def owner_slots(flat_codes, devices, capacity, rows_own):
    owner = flat_codes // rows_own
    order = jnp.argsort(owner, stable=True)
    ranked = owner[order]
    first = jnp.searchsorted(ranked, jnp.arange(devices, dtype=jnp.int32))
    place = jnp.arange(flat_codes.shape[0], dtype=jnp.int32) - first[ranked]
    return jnp.zeros_like(flat_codes).at[order].set(ranked * capacity + place)


def on_device(
    pixels,
    valid_mask,
    size_groups,
    code_index,
    w_pixel,
    w_res,
    w_scale,
    w_latent,
    norm_gains,
    moment_pixel,
    moment_res,
    moment_scale,
    moment_latent,
    moment_gains,
    second_pixel,
    second_res,
    second_scale,
    second_latent,
    second_gains,
    ema_counts,
    ema_sums,
):
    canv = size_groups.shape[0]
    n_outer = lax.axis_size("dp")
    n_inner = lax.axis_size("fsdp")
    devices = n_outer * n_inner
    latent_all = code_index.shape[1] * devices
    rows = ema_sums.shape[0]
    flat_codes = code_index.reshape(-1)
    capacity = max(2, 2 * flat_codes.shape[0] // devices)
    slot = owner_slots(flat_codes, devices, capacity, rows)
    local_row = flat_codes % rows
    geom = geometry(size_groups, SIDE, C)
    mask = valid_mask.astype(jnp.float32)
    total_valid = lax.psum(jnp.sum(mask), ("dp", "fsdp"))
    book = (ema_sums / ema_counts[:, None]).astype(jnp.bfloat16)
    wanted = jnp.full((devices * capacity,), -1, jnp.int32).at[slot].set(local_row)
    wanted = wanted.reshape(n_outer, n_inner, capacity)
    asked = lax.all_to_all(
        lax.all_to_all(wanted, "dp", split_axis=0, concat_axis=0, tiled=True),
        "fsdp",
        split_axis=1,
        concat_axis=1,
        tiled=True,
    )
    answer = jnp.take(book, jnp.maximum(asked, 0), axis=0)
    replies = lax.all_to_all(
        lax.all_to_all(answer, "dp", split_axis=0, concat_axis=0, tiled=True),
        "fsdp",
        split_axis=1,
        concat_axis=1,
        tiled=True,
    )
    picked_rows = replies.reshape(devices * capacity, -1)[slot].reshape(
        code_index.shape + (book.shape[1],)
    )
    q_cum = jnp.cumsum(picked_rows.astype(jnp.float32), axis=0)
    patch_in = fetch(w_pixel[0])
    field = jnp.dot(pixels, patch_in, preferred_element_type=jnp.float32).reshape(
        canv, SIDE, SIDE, C
    )
    enc_taps = (fetch(w_res[0]).reshape(9, C, C), fetch(w_res[1]).reshape(9, C, C))
    field, kept_enc = block_forward(field, enc_taps, norm_gains, 0, geom)
    e_four = to_depth(field.astype(jnp.bfloat16))
    w_down = fetch(w_scale[0])
    hidden = jnp.dot(e_four, w_down, preferred_element_type=jnp.float32)
    s_one = jax.nn.silu(hidden).astype(jnp.bfloat16)
    w_proj = fetch(w_latent[0])
    latent = jnp.dot(s_one, w_proj, preferred_element_type=jnp.float32)
    diff = latent[None] - q_cum
    commit = jnp.sum(diff * diff)
    shift = q_cum[DEPTH - 1] - latent
    quant = (latent + shift).astype(jnp.bfloat16)
    w_back = fetch(w_latent[1])
    inner = along_cols(quant, w_back)
    s_two = jax.nn.silu(inner).astype(jnp.bfloat16)
    w_up = fetch(w_scale[1])
    upper = along_cols(s_two, w_up)
    dec_field = from_depth(upper, canv, SIDE)
    dec_taps = (fetch(w_res[2]).reshape(9, C, C), fetch(w_res[3]).reshape(9, C, C))
    dec_field, kept_dec = block_forward(dec_field, dec_taps, norm_gains, 2, geom)
    outer = jax.nn.silu(dec_field).astype(jnp.bfloat16).reshape(-1, C)
    w_head = fetch(w_pixel[1])
    recon = along_cols(outer, w_head)
    err = recon - pixels.astype(jnp.float32)
    smooth = jnp.sqrt(err * err + 1.0)
    l1_local = jnp.sum(mask * (smooth - 1.0))
    grad_rec = (mask * err / smooth / total_valid).astype(jnp.bfloat16)
    d_head = along_rows(grad_rec, outer)
    head_b = backward_copy(w_pixel[1], w_head)
    d_outer = jnp.dot(grad_rec, head_b, preferred_element_type=jnp.float32)
    d_dec = (d_outer * silu_slope(dec_field.reshape(-1, C))).reshape(dec_field.shape)
    dec_b = (backward_copy(w_res[2], dec_taps[0]), backward_copy(w_res[3], dec_taps[1]))
    d_dec, dec_grads, dec_gain = block_backward(d_dec, kept_dec, dec_b, norm_gains, 2, geom)
    d_upper = to_depth(d_dec).astype(jnp.bfloat16)
    d_up = along_rows(d_upper, s_two)
    up_b = backward_copy(w_scale[1], w_up)
    d_s_two = jnp.dot(d_upper, up_b, preferred_element_type=jnp.float32)
    d_inner = (d_s_two * silu_slope(inner)).astype(jnp.bfloat16)
    d_back = along_rows(d_inner, quant)
    back_b = backward_copy(w_latent[1], w_back)
    d_quant = jnp.dot(d_inner, back_b, preferred_element_type=jnp.float32)
    d_latent = d_quant + 2.0 * COMMIT_WEIGHT / (latent_all * ZD) * jnp.sum(diff, axis=0)
    d_latent = d_latent.astype(jnp.bfloat16)
    d_proj = along_rows(s_one, d_latent)
    proj_b = backward_copy(w_latent[0], w_proj)
    d_s_one = along_cols(d_latent, proj_b)
    d_hidden = (d_s_one * silu_slope(hidden)).astype(jnp.bfloat16)
    d_down = along_rows(e_four, d_hidden)
    down_b = backward_copy(w_scale[0], w_down)
    d_e_four = along_cols(d_hidden, down_b)
    d_enc = from_depth(d_e_four, canv, SIDE)
    enc_b = (backward_copy(w_res[0], enc_taps[0]), backward_copy(w_res[1], enc_taps[1]))
    d_enc, enc_grads, enc_gain = block_backward(d_enc, kept_enc, enc_b, norm_gains, 0, geom)
    d_first = d_enc.reshape(-1, C).astype(jnp.bfloat16)
    d_patch = along_rows(pixels, d_first)
    grad_pixel = jnp.stack([reduce_grad(d_patch), reduce_grad(d_head)])
    grad_res = jnp.stack(
        [
            reduce_grad(enc_grads[0]),
            reduce_grad(enc_grads[1]),
            reduce_grad(dec_grads[0]),
            reduce_grad(dec_grads[1]),
        ]
    )
    grad_scale = jnp.stack([reduce_grad(d_down), reduce_grad(d_up)])
    grad_latent = jnp.stack([reduce_grad(d_proj), reduce_grad(d_back)])
    gain_local = jnp.stack(
        [
            enc_gain[0],
            enc_gain[1],
            dec_gain[0],
            dec_gain[1],
            enc_gain[2],
            enc_gain[3],
            dec_gain[2],
            dec_gain[3],
        ]
    )
    grad_gains, smooth_sum, commit_sum = lax.psum((gain_local, l1_local, commit), ("dp", "fsdp"))
    shard_squares = jnp.sum(grad_pixel * grad_pixel) + jnp.sum(grad_res * grad_res)
    shard_squares = (
        shard_squares + jnp.sum(grad_scale * grad_scale) + jnp.sum(grad_latent * grad_latent)
    )
    total_squares = lax.psum(shard_squares, ("dp", "fsdp")) + jnp.sum(grad_gains * grad_gains)
    norm = jnp.sqrt(total_squares)
    factor = CLIP_AT / jnp.maximum(norm, CLIP_AT)
    groups_all = [
        (w_pixel, moment_pixel, second_pixel, grad_pixel),
        (w_res, moment_res, second_res, grad_res),
        (w_scale, moment_scale, second_scale, grad_scale),
        (w_latent, moment_latent, second_latent, grad_latent),
    ]
    outputs = [jnp.stack([smooth_sum, total_valid, commit_sum]), norm.reshape(1)]
    for weight, moment, second, grad in groups_all:
        weight_new, moment_new, second_new = adam_step(
            weight, moment, second, grad * factor, WEIGHT_RATE
        )
        outputs += [weight_new, moment_new, second_new, weight_new.astype(jnp.bfloat16)]
    outputs += list(
        adam_step(norm_gains, moment_gains, second_gains, grad_gains * factor, GAIN_RATE)
    )
    prev = jnp.concatenate([jnp.zeros_like(q_cum[:1]), q_cum[:-1]], axis=0)
    resid = (latent[None] - prev).astype(jnp.bfloat16).reshape(-1, ZD)
    block_len = min(K, 2048)

    def code_block(start):
        onehot = (
            flat_codes[:, None] == start + jnp.arange(block_len, dtype=jnp.int32)[None, :]
        ).astype(jnp.bfloat16)
        return (along_rows(onehot, resid), jnp.sum(onehot, axis=0, dtype=jnp.float32))

    sums_all, counts_all = lax.map(code_block, jnp.arange(0, K, block_len, dtype=jnp.int32))
    sums_all = sums_all.reshape(K, ZD)
    counts_all = counts_all.reshape(K)
    sums_total, counts_total = lax.psum((sums_all, counts_all), ("dp", "fsdp"))
    start_row = lax.axis_index(("dp", "fsdp")) * rows
    my_sums = lax.dynamic_slice_in_dim(sums_total, start_row, rows, 0)
    my_counts = lax.dynamic_slice_in_dim(counts_total, start_row, rows, 0)
    counts_new = EMA_DECAY * ema_counts + (1.0 - EMA_DECAY) * my_counts
    sums_new = EMA_DECAY * ema_sums + (1.0 - EMA_DECAY) * my_sums
    book_new = sums_new / counts_new[:, None]
    outputs += [counts_new, sums_new, book_new, book_new.astype(jnp.bfloat16)]
    return tuple(outputs)


def solution(mesh):
    placed = (
        P(("dp", "fsdp"), None),
        P(("dp", "fsdp"), None),
        P(("dp", "fsdp")),
        P(None, ("dp", "fsdp")),
        P(None, "fsdp", "dp"),
        P(None, "fsdp", "dp"),
        P(None, "fsdp", "dp"),
        P(None, "fsdp", "dp"),
        P(),
        P(None, "fsdp", "dp"),
        P(None, "fsdp", "dp"),
        P(None, "fsdp", "dp"),
        P(None, "fsdp", "dp"),
        P(),
        P(None, "fsdp", "dp"),
        P(None, "fsdp", "dp"),
        P(None, "fsdp", "dp"),
        P(None, "fsdp", "dp"),
        P(),
        P(("dp", "fsdp")),
        P(("dp", "fsdp"), None),
    )
    return jax.shard_map(
        on_device,
        mesh=mesh,
        in_specs=placed,
        out_specs=(
            P(),
            P(),
            P(None, "fsdp", "dp"),
            P(None, "fsdp", "dp"),
            P(None, "fsdp", "dp"),
            P(None, "fsdp", "dp"),
            P(None, "fsdp", "dp"),
            P(None, "fsdp", "dp"),
            P(None, "fsdp", "dp"),
            P(None, "fsdp", "dp"),
            P(None, "fsdp", "dp"),
            P(None, "fsdp", "dp"),
            P(None, "fsdp", "dp"),
            P(None, "fsdp", "dp"),
            P(None, "fsdp", "dp"),
            P(None, "fsdp", "dp"),
            P(None, "fsdp", "dp"),
            P(None, "fsdp", "dp"),
            P(),
            P(),
            P(),
            P(("dp", "fsdp")),
            P(("dp", "fsdp"), None),
            P(("dp", "fsdp"), None),
            P(("dp", "fsdp"), None),
        ),
        check_vma=False,
    )
```

profile of v0, /device:TPU:12, one launch (start us, length us, event | category | flops | bytes accessed | tf_op | source)
XLA Modules:
  0.0 1944.9 jit_solution(17899605121491176382)
XLA Ops:
  11.5 22.5 %all-gather.31.cloned.1.call-done = bf16[1,1152,512]{1,2,0:T(8,128)(2,1)} async-done(((bf16[1,1152,64]{1,2,0:T(8,128)(2,1)}), bf16[1,1152,512]{1,2,0:T(8,128)(2,1)}) %all-gather.31.cloned.1.call-update) | async-done | bytes 1179664 | tf_op jit(solution)/shard_map/all_gather | solution.py:150
  36.5 22.2 %all-gather.35.cloned.1.call-done = bf16[1,1152,512]{1,2,0:T(8,128)(2,1)} async-done(((bf16[1,1152,64]{1,2,0:T(8,128)(2,1)}), bf16[1,1152,512]{1,2,0:T(8,128)(2,1)}) %all-gather.35.cloned.1.call-update) | async-done | bytes 1179664 | tf_op jit(solution)/shard_map/all_gather | solution.py:150
  61.2 15.9 all-gather.6
  77.2 16.3 all-gather.12
  119.3 15.9 fusion.437
  208.5 29.5 %all-gather.10 = bf16[1,128,256]{1,2,0:T(8,128)(2,1)S(1)} all-gather(bf16[1,128,32]{1,2,0:T(8,128)(2,1)S(1)} %get-tuple-element.455), channel_id=12, replica_groups=mesh['dp'=8,'fsdp'=4] {'dp'}, dimensions={2}, use_global_device_ids=true | all-gather | bytes 73728 | tf_op jit(solution)/shard_map/all_gather | solution.py:150
  471.4 41.4 %psum.50 = f32[]{:T(128)} all-reduce(f32[]{:T(128)} %get-tuple-element.298), channel_id=1, replica_groups=mesh['dp'=8,'fsdp'=4] {'dp','fsdp'}, use_global_device_ids=true, to_apply=%region_27.30 | all-reduce | flops 1 | bytes 8 | tf_op jit(solution)/shard_map/psum | solution.py:217
  795.2 49.7 %while.36 = (s32[]{:T(128)}, f32[8,2048,256]{2,1,0:T(8,128)}, f32[8,2048]{1,0:T(8,128)S(1)}, s32[4,256]{1,0:T(4,128)S(1)}, s32[8]{0:T(128)S(1)}, /*index=5*/bf16[1024,256]{1,0:T(8,128)(2,1)S(1)}, s32[]{:T(128)}, s32[]{:T(128)}) while((s32[]{:T(128)}, f32[8,2048,256]{2,1,0:T(8,128)}, f32[8,2048]{1,0:T(8,128)S(1)}, s32[4,256]{1,0:T(4,128)S(1)}, ...), condition=%wide.region_84.87_spmd, body=%wide.region_82.86_spmd.sunk | while | flops 1084227584 | bytes 2687093 | solution.py:355
  851.7 95.4 %reduce-scatter.45.cloned.1.call-done = f32[1152,512]{1,0:T(8,128)} async-done(((f32[4608,512]{1,0:T(8,128)}), f32[1152,512]{1,0:T(8,128)}) %reduce-scatter.45.cloned.1.call-update) | async-done | bytes 2359312 | tf_op jit(solution)/shard_map/reduce_scatter | solution.py:159
  950.2 94.9 %reduce-scatter.47.cloned.1.call-done = f32[1152,512]{1,0:T(8,128)} async-done(((f32[4608,512]{1,0:T(8,128)}), f32[1152,512]{1,0:T(8,128)}) %reduce-scatter.47.cloned.1.call-update) | async-done | bytes 2359312 | tf_op jit(solution)/shard_map/reduce_scatter | solution.py:159
  1048.3 95.0 %reduce-scatter.49.cloned.1.call-done = f32[1152,512]{1,0:T(8,128)} async-done(((f32[4608,512]{1,0:T(8,128)}), f32[1152,512]{1,0:T(8,128)}) %reduce-scatter.49.cloned.1.call-update) | async-done | bytes 2359312 | tf_op jit(solution)/shard_map/reduce_scatter | solution.py:159
  1146.4 94.9 %reduce-scatter.51.cloned.1.call-done = f32[1152,512]{1,0:T(8,128)} async-done(((f32[4608,512]{1,0:T(8,128)}), f32[1152,512]{1,0:T(8,128)}) %reduce-scatter.51.cloned.1.call-update) | async-done | bytes 2359312 | tf_op jit(solution)/shard_map/reduce_scatter | solution.py:159
  1245.8 25.0 %reduce-scatter.77.cloned.1.call-done = f32[32,128]{1,0:T(8,128)} async-done(((f32[256,128]{1,0:T(8,128)}), f32[32,128]{1,0:T(8,128)}) %reduce-scatter.77.cloned.1.call-update) | async-done | bytes 16400
  1271.7 30.3 %reduce-scatter.79.cloned.1.call-done = f32[32,128]{1,0:T(8,128)} async-done(((f32[256,128]{1,0:T(8,128)}), f32[32,128]{1,0:T(8,128)}) %reduce-scatter.79.cloned.1.call-update) | async-done | bytes 16400
  1303.5 30.4 %reduce-scatter.43.cloned.1.call-done = f32[192,64]{0,1:T(8,128)} async-done(((f32[192,512]{0,1:T(8,128)}), f32[192,64]{0,1:T(8,128)}) %reduce-scatter.43.cloned.1.call-update) | async-done | bytes 49168 | tf_op jit(solution)/shard_map/reduce_scatter | solution.py:160
  1334.0 31.9 %reduce-scatter.41.cloned.1.call-done = f32[192,64]{0,1:T(8,128)} async-done(((f32[192,512]{0,1:T(8,128)}), f32[192,64]{0,1:T(8,128)}) %reduce-scatter.41.cloned.1.call-update) | async-done | bytes 49168 | tf_op jit(solution)/shard_map/reduce_scatter | solution.py:160
  1367.4 288.5 %all-reduce.41.cloned.1.call-done = (f32[16384]{0:T(1024)}, f32[16384,256]{1,0:T(8,128)}) async-done(((f32[16384]{0:T(1024)}, f32[16384,256]{1,0:T(8,128)}), (f32[16384]{0:T(1024)}, f32[16384,256]{1,0:T(8,128)})) %all-reduce.41.cloned.1.call-update) | async-done | bytes 16842768 | tf_op jit(solution)/shard_map/psum | solution.py:358
  1658.8 28.4 %reduce-scatter.75.cloned.1.call-done = f32[64,512]{1,0:T(8,128)} async-done(((f32[512,512]{1,0:T(8,128)}), f32[64,512]{1,0:T(8,128)}) %reduce-scatter.75.cloned.1.call-update) | async-done | bytes 131088
  1687.2 33.6 %reduce-scatter.73.cloned.1.call-done = f32[64,512]{1,0:T(8,128)} async-done(((f32[512,512]{1,0:T(8,128)}), f32[64,512]{1,0:T(8,128)}) %reduce-scatter.73.cloned.1.call-update) | async-done | bytes 131088
  1722.4 35.2 %reduce-scatter.65.cloned.1.call-done = f32[64,1152]{1,0:T(8,128)} async-done(((f32[512,1152]{1,0:T(8,128)}), f32[64,1152]{1,0:T(8,128)}) %reduce-scatter.65.cloned.1.call-update) | async-done | bytes 294928
  1757.6 37.8 %reduce-scatter.67.cloned.1.call-done = f32[64,1152]{1,0:T(8,128)} async-done(((f32[512,1152]{1,0:T(8,128)}), f32[64,1152]{1,0:T(8,128)}) %reduce-scatter.67.cloned.1.call-update) | async-done | bytes 294928
  1795.4 37.7 %reduce-scatter.69.cloned.1.call-done = f32[64,1152]{1,0:T(8,128)} async-done(((f32[512,1152]{1,0:T(8,128)}), f32[64,1152]{1,0:T(8,128)}) %reduce-scatter.69.cloned.1.call-update) | async-done | bytes 294928
  1833.0 37.8 %reduce-scatter.71.cloned.1.call-done = f32[64,1152]{1,0:T(8,128)} async-done(((f32[512,1152]{1,0:T(8,128)}), f32[64,1152]{1,0:T(8,128)}) %reduce-scatter.71.cloned.1.call-update) | async-done | bytes 294928
  1875.8 44.7 %all-reduce.37 = (f32[1]{0:T(128)}, f32[1]{0:T(128)}, f32[]{:T(128)}, f32[8,512]{1,0:T(8,128)}) all-reduce(f32[1]{0:T(128)} %bitcast.179, f32[1]{0:T(128)} %bitcast.177, f32[]{:T(128)S(6)} %add.1351, f32[8,512]{1,0:T(8,128)} %stack.107), channel_id=1, replica_groups=mesh['dp'=8,'fsdp'=4] {'dp','fsdp'}, use_global_device_ids=true, to_apply=%region_29.32 | all-reduce | flops 4099 | bytes 32792 | tf_op jit(solution)/shard_map/psum | solution.py:322
  (1059 shorter events, 722.9 us)
Async XLA Ops:
  10.9 314.8 %all-gather.47.cloned.1.call-start = ((), (), s32[]{:S(2)}) async-start(), calls=%async_computation.42 | async-start | bytes 1327104 | tf_op jit(solution)/shard_map/all_gather | solution.py:150
  11.5 322.0 %all-gather.33.cloned.1.call-start = ((), (), s32[]{:S(2)}) async-start(), calls=%async_computation.35 | async-start | bytes 5898240 | tf_op jit(solution)/shard_map/all_gather | solution.py:151
  36.4 333.2 %all-gather.37.cloned.1.call-start = ((), (), s32[]{:S(2)}) async-start(), calls=%async_computation.37 | async-start | bytes 5898240 | tf_op jit(solution)/shard_map/all_gather | solution.py:151
  61.1 323.2 %all-gather.39.cloned.1.call-start = ((), (), s32[]{:S(2)}) async-start(), calls=%async_computation.38 | async-start | bytes 2621440 | tf_op jit(solution)/shard_map/all_gather | solution.py:151
  77.2 311.2 %all-gather.41.cloned.1.call-start = ((), (), s32[]{:S(2)}) async-start(), calls=%async_computation.39 | async-start | bytes 2621440 | tf_op jit(solution)/shard_map/all_gather | solution.py:151
  93.5 331.1 %all-gather.45.cloned.1.call-start = ((), (), s32[]{:S(2)}) async-start(), calls=%async_computation.41 | async-start | bytes 5898240 | tf_op jit(solution)/shard_map/all_gather | solution.py:151
  266.1 184.8 %all-gather.49.cloned.1.call-start = ((), (), s32[]{:S(2)}) async-start(), calls=%async_computation.43 | async-start | bytes 5898240 | tf_op jit(solution)/shard_map/all_gather | solution.py:151
  325.8 461.3 %reduce-scatter.57.cloned.1.call-start = ((), (), s32[]{:S(2)}) async-start(), calls=%async_computation.32 | async-start | bytes 655360 | tf_op jit(solution)/shard_map/reduce_scatter | solution.py:159
  607.9 181.0 %reduce-scatter.59.cloned.1.call-start = ((), (), s32[]{:S(2)}) async-start(), calls=%async_computation.33 | async-start | bytes 655360 | tf_op jit(solution)/shard_map/reduce_scatter | solution.py:159
  714.1 233.0 %reduce-scatter.45.cloned.1.call-start = ((), (), s32[]{:S(2)}) async-start(), calls=%async_computation.26 | async-start | bytes 11796480 | tf_op jit(solution)/shard_map/reduce_scatter | solution.py:159
  730.8 314.3 %reduce-scatter.47.cloned.1.call-start = ((), (), s32[]{:S(2)}) async-start(), calls=%async_computation.27 | async-start | bytes 11796480 | tf_op jit(solution)/shard_map/reduce_scatter | solution.py:159
  748.0 395.2 %reduce-scatter.49.cloned.1.call-start = ((), (), s32[]{:S(2)}) async-start(), calls=%async_computation.28 | async-start | bytes 11796480 | tf_op jit(solution)/shard_map/reduce_scatter | solution.py:159
  769.9 471.4 %reduce-scatter.51.cloned.1.call-start = ((), (), s32[]{:S(2)}) async-start(), calls=%async_computation.29 | async-start | bytes 11796480 | tf_op jit(solution)/shard_map/reduce_scatter | solution.py:159
  787.0 483.9 %reduce-scatter.77.cloned.1.call-start = ((), (), s32[]{:S(2)}) async-start(), calls=%async_computation.52 | async-start | bytes 147456
  788.8 513.2 %reduce-scatter.79.cloned.1.call-start = ((), (), s32[]{:S(2)}) async-start(), calls=%async_computation.53 | async-start | bytes 147456
  790.6 543.4 %reduce-scatter.43.cloned.1.call-start = ((), (), s32[]{:S(2)}) async-start(), calls=%async_computation.25 | async-start | bytes 589824 | tf_op jit(solution)/shard_map/reduce_scatter | solution.py:160
  792.7 573.2 %reduce-scatter.41.cloned.1.call-start = ((), (), s32[]{:S(2)}) async-start(), calls=%async_computation.24 | async-start | bytes 589824 | tf_op jit(solution)/shard_map/reduce_scatter | solution.py:160
  794.8 861.0 %all-reduce.41.cloned.1.call-start = ((), (), s32[]{:S(2)}) async-start(), calls=%async_computation.54 | async-start | bytes 33685504 | tf_op jit(solution)/shard_map/psum | solution.py:358
  845.6 841.6 %reduce-scatter.75.cloned.1.call-start = ((), (), s32[]{:S(2)}) async-start(), calls=%async_computation.51 | async-start | bytes 1179648
  848.2 872.5 %reduce-scatter.73.cloned.1.call-start = ((), (), s32[]{:S(2)}) async-start(), calls=%async_computation.50 | async-start | bytes 1179648
  851.6 905.9 %reduce-scatter.65.cloned.1.call-start = ((), (), s32[]{:S(2)}) async-start(), calls=%async_computation.46 | async-start | bytes 2654208
  950.1 845.2 %reduce-scatter.67.cloned.1.call-start = ((), (), s32[]{:S(2)}) async-start(), calls=%async_computation.47 | async-start | bytes 2654208
  1048.2 784.8 %reduce-scatter.69.cloned.1.call-start = ((), (), s32[]{:S(2)}) async-start(), calls=%async_computation.48 | async-start | bytes 2654208
  1146.4 724.5 %reduce-scatter.71.cloned.1.call-start = ((), (), s32[]{:S(2)}) async-start(), calls=%async_computation.49 | async-start | bytes 2654208
  (236 other events, 3963.7 us)
Sparse Core Ops, SparseCore 0:
  112.1 56.5 all-gather.32
  171.0 57.1 all-gather.36
  230.0 35.1 all-gather.38
  267.0 40.4 all-gather.40
  310.0 57.5 all-gather.44
  369.3 57.0 all-gather.48
  667.4 30.8 reduce-scatter.62
  707.1 30.5 reduce-scatter.60
  740.6 52.6 reduce-scatter.54
  796.3 52.6 reduce-scatter.52
  852.0 94.9 reduce-scatter.44
  950.0 95.0 reduce-scatter.46
  1048.2 95.0 reduce-scatter.48
  1146.2 95.0 reduce-scatter.50
  1273.8 28.2 reduce-scatter.78
  1304.9 29.0 reduce-scatter.42
  1336.8 29.0 reduce-scatter.40
  1372.9 282.9 all-reduce.40
  1658.6 28.5 reduce-scatter.74
  1689.9 30.8 reduce-scatter.72
  1723.1 34.4 reduce-scatter.64
  1759.9 35.4 reduce-scatter.66
  1797.5 35.4 reduce-scatter.68
  1835.4 35.4 reduce-scatter.70
  (7 shorter events, 168.1 us)
where the time goes:
time: 1960 us; the launch traced here: 1940 us
  waiting for transfers between devices  1050 us (54%)
  matrix products  256 us (13%)
  blocking collectives  237 us (12%)
  local copies, waits for them, and re-layouts  188 us (10%)
  other arithmetic  170 us (9%)
  between operations  24.2 us (1%)
  starting transfers between devices  22.2 us (1%)
    reduce_scatter x8, waiting for transfers between devices, reduce_grad(): rows = lax.psum_scatter(full, 'fsdp', scatter_dimension=0, tiled=True)  381 us
    psum x1, waiting for transfers between devices, on_device(): sums_total, counts_total = lax.psum((sums_all, counts_all), ('dp', 'fsdp'))  288 us
    unnamed x41, waiting for transfers between devices  268 us
    all_gather x6, blocking collectives, fetch(): cols = lax.all_gather(shard.astype(jnp.bfloat16), 'dp', axis=1, tiled=True)  106 us
    dot_general x49, matrix products, along_rows(): lax.dot_general(left, right, (((0,), (0,)), ((), ())), preferred_element_...  103 us
    dot_general x41, matrix products, along_cols(): lax.dot_general(left, right, (((1,), (1,)), ((), ())), preferred_element_...  88.1 us
    reduce_scatter x2, waiting for transfers between devices, reduce_grad(): return lax.psum_scatter(rows, 'dp', scatter_dimension=1, tiled=True)  62.3 us
    unnamed x467, local copies, waits for them, and re-layouts  60.6 us
  transfers between devices with their start and end apart: 35, of which 19 were waited for; matrix products, arithmetic and copies ran while one was open for 24% of the time, Pallas kernels for 0%

commit v1 on v0

--- a/solution.py
+++ b/solution.py
@@ -148,7 +148,38 @@
 
 def fetch(shard):
     cols = lax.all_gather(shard.astype(jnp.bfloat16), "dp", axis=1, tiled=True)
-    return lax.all_gather(cols, "fsdp", axis=0, tiled=True)
+
+    def run_values_now(inp, ax_name):
+        fresh = lax.axis_size(ax_name)
+        field_out, u_next, v_next = (fresh, lax.axis_index(ax_name), inp.shape[0])
+        samples = tuple((j * field_out if i == 0 else j for i, j in enumerate(inp.shape)))
+        r1 = lax.dynamic_update_slice_in_dim(
+            jnp.zeros(samples, inp.dtype), inp, u_next * v_next, axis=0
+        )
+        local_out = tile_out = inp
+        dev_i = 1
+        while dev_i < field_out // 2 + 1:
+            local_out = lax.ppermute(
+                local_out,
+                axis_name=ax_name,
+                perm=tuple(((i, (i + 1) % field_out) for i in range(field_out))),
+            )
+            r1 = lax.dynamic_update_slice_in_dim(
+                r1, local_out, (u_next - dev_i) % field_out * v_next, axis=0
+            )
+            if 2 * dev_i < field_out:
+                tile_out = lax.ppermute(
+                    tile_out,
+                    axis_name=ax_name,
+                    perm=tuple(((i, (i - 1) % field_out) for i in range(field_out))),
+                )
+                r1 = lax.dynamic_update_slice_in_dim(
+                    r1, tile_out, (u_next + dev_i) % field_out * v_next, axis=0
+                )
+            dev_i += 1
+        return r1
+
+    return run_values_now(cols, "fsdp")
 
 
 def backward_copy(shard, ready):

time: 1960 us -> 2320 us (1.18)
  waiting for transfers between devices: 1050 us -> 1220 us
  local copies, waits for them, and re-layouts: 188 us -> 311 us
  matrix products: 256 us -> 331 us
  blocking collectives: 237 us -> 178 us
  starting transfers between devices: 22.2 us -> 65.3 us
    ppermute x0 -> x30, waiting for transfers between devices: none -> 220 us  [the longest x20 173 us: run_values_now(): lax.ppermute(local_out, axis_name=ax_name, perm=tuple(((i, (i + 1) % fiel...]
    dynamic_update_slice x0 -> x39, local copies, waits for them, and re-layouts: none -> 72.8 us  [the longest x19 38.7 us: run_values_now(): lax.dynamic_update_slice_in_dim(r1, local_out, (u_next - dev_i) % field_o...]
    dot_general x41, matrix products: 88.1 us -> 138 us  [along_cols(): lax.dot_general(left, right, (((1,), (1,)), ((), ())), preferred_element_...]
    all_gather x4 -> x0, blocking collectives: 44.8 us -> none  [fetch(): return lax.all_gather(cols, 'fsdp', axis=0, tiled=True)]
    all_gather x4, waiting for transfers between devices: 44.7 us -> 0.01 us  [fetch(): cols = lax.all_gather(shard.astype(jnp.bfloat16), 'dp', axis=1, tiled=True)]
    ppermute x0 -> x30, starting transfers between devices: none -> 44.6 us  [the longest x20 27.2 us: run_values_now(): lax.ppermute(local_out, axis_name=ax_name, perm=tuple(((i, (i + 1) % fiel...]
    unnamed x467 -> x505, local copies, waits for them, and re-layouts: 60.6 us -> 58.9 us
    unnamed x41 -> x35, waiting for transfers between devices: 268 us -> 267 us
  transfers between devices with their start and end apart: 35 -> 59, of which waited for: 19 -> 26; matrix products, arithmetic and copies ran while one was open for 24% -> 26% of each run, Pallas kernels for 0% -> 0%
where the time goes in v1:
time: 2320 us; the launch traced here: 2300 us
  waiting for transfers between devices  1220 us (53%)
  matrix products  331 us (14%)
  local copies, waits for them, and re-layouts  311 us (13%)
  blocking collectives  178 us (8%)
  other arithmetic  171 us (7%)
  starting transfers between devices  65.3 us (3%)
  between operations  24.4 us (1%)
    reduce_scatter x8, waiting for transfers between devices, reduce_grad(): rows = lax.psum_scatter(full, 'fsdp', scatter_dimension=0, tiled=True)  386 us
    psum x1, waiting for transfers between devices, on_device(): sums_total, counts_total = lax.psum((sums_all, counts_all), ('dp', 'fsdp'))  288 us
    unnamed x35, waiting for transfers between devices  267 us
    ppermute x20, waiting for transfers between devices, run_values_now(): lax.ppermute(local_out, axis_name=ax_name, perm=tuple(((i, (i + 1) % fiel...  173 us
    dot_general x41, matrix products, along_cols(): lax.dot_general(left, right, (((1,), (1,)), ((), ())), preferred_element_...  138 us
    dot_general x49, matrix products, along_rows(): lax.dot_general(left, right, (((0,), (0,)), ((), ())), preferred_element_...  103 us
    all_gather x6, blocking collectives, fetch(): cols = lax.all_gather(shard.astype(jnp.bfloat16), 'dp', axis=1, tiled=True)  91.2 us
    dot_general x36, matrix products, conv_forward(): jnp.dot(piece, taps[index], preferred_element_type=jnp.float32)  62.4 us
  transfers between devices with their start and end apart: 59, of which 26 were waited for; matrix products, arithmetic and copies ran while one was open for 26% of the time, Pallas kernels for 0%

profile of v1, /device:TPU:12, one launch (start us, length us, event | category | flops | bytes accessed | tf_op | source)
XLA Modules:
  0.0 2304.5 jit_solution(10111510585663786556)
XLA Ops:
  365.2 44.4 %collective-permute-done.6 = bf16[1152,512]{1,0:T(8,128)(2,1)} collective-permute-done((bf16[1152,512]{1,0:T(8,128)(2,1)}, bf16[1152,512]{1,0:T(8,128)(2,1)}, u32[]{:S(2)}, u32[]{:S(2)}) %collective-permute-start.6) | collective-permute-done | bytes 1179680 | tf_op jit(solution)/shard_map/ppermute | solution.py:162
  417.3 42.8 %collective-permute-done.21 = bf16[1152,512]{1,0:T(8,128)(2,1)} collective-permute-done((bf16[1152,512]{1,0:T(8,128)(2,1)}, bf16[1152,512]{1,0:T(8,128)(2,1)}, u32[]{:S(2)}, u32[]{:S(2)}) %collective-permute-start.21) | collective-permute-done | bytes 1179680 | tf_op jit(solution)/shard_map/ppermute | solution.py:162
  488.3 22.3 collective-permute-done.22
  511.7 24.2 %collective-permute-done.25 = bf16[1152,512]{1,0:T(8,128)(2,1)S(1)} collective-permute-done((bf16[1152,512]{1,0:T(8,128)(2,1)S(1)}, bf16[1152,512]{1,0:T(8,128)(2,1)S(1)}, u32[]{:S(2)}, u32[]{:S(2)}) %collective-permute-start.25) | collective-permute-done | bytes 1179680 | tf_op jit(solution)/shard_map/ppermute | solution.py:171
  537.0 24.2 %collective-permute-done.5 = bf16[1152,512]{1,0:T(8,128)(2,1)S(1)} collective-permute-done((bf16[1152,512]{1,0:T(8,128)(2,1)}, bf16[1152,512]{1,0:T(8,128)(2,1)S(1)}, u32[]{:S(2)}, u32[]{:S(2)}) %collective-permute-start.5) | collective-permute-done | bytes 1179680 | tf_op jit(solution)/shard_map/ppermute | solution.py:162
  561.1 25.3 %collective-permute-done.23 = bf16[1152,512]{1,0:T(8,128)(2,1)S(1)} collective-permute-done((bf16[1152,512]{1,0:T(8,128)(2,1)}, bf16[1152,512]{1,0:T(8,128)(2,1)S(1)}, u32[]{:S(2)}, u32[]{:S(2)}) %collective-permute-start.23) | collective-permute-done | bytes 1179680 | tf_op jit(solution)/shard_map/ppermute | solution.py:162
  774.8 41.6 %psum.50 = f32[]{:T(128)} all-reduce(f32[]{:T(128)} %get-tuple-element.298), channel_id=1, replica_groups=mesh['dp'=8,'fsdp'=4] {'dp','fsdp'}, use_global_device_ids=true, to_apply=%region_27.30 | all-reduce | flops 1 | bytes 8 | tf_op jit(solution)/shard_map/psum | solution.py:248
  1150.2 49.5 %while.36 = (s32[]{:T(128)}, f32[8,2048,256]{2,1,0:T(8,128)}, f32[8,2048]{1,0:T(8,128)S(1)}, s32[4,256]{1,0:T(4,128)S(1)}, s32[8]{0:T(128)S(1)}, /*index=5*/bf16[1024,256]{1,0:T(8,128)(2,1)S(1)}, s32[]{:T(128)}, s32[]{:T(128)}) while((s32[]{:T(128)}, f32[8,2048,256]{2,1,0:T(8,128)}, f32[8,2048]{1,0:T(8,128)S(1)}, s32[4,256]{1,0:T(4,128)S(1)}, ...), condition=%wide.region_84.87_spmd, body=%wide.region_82.86_spmd.sunk | while | flops 1084227584 | bytes 2687093 | solution.py:386
  1211.7 95.5 %reduce-scatter.45.cloned.1.call-done = f32[1152,512]{1,0:T(8,128)} async-done(((f32[4608,512]{1,0:T(8,128)}), f32[1152,512]{1,0:T(8,128)}) %reduce-scatter.45.cloned.1.call-update) | async-done | bytes 2359312 | tf_op jit(solution)/shard_map/reduce_scatter | solution.py:190
  1310.7 94.6 %reduce-scatter.47.cloned.1.call-done = f32[1152,512]{1,0:T(8,128)} async-done(((f32[4608,512]{1,0:T(8,128)}), f32[1152,512]{1,0:T(8,128)}) %reduce-scatter.47.cloned.1.call-update) | async-done | bytes 2359312 | tf_op jit(solution)/shard_map/reduce_scatter | solution.py:190
  1408.4 95.0 %reduce-scatter.49.cloned.1.call-done = f32[1152,512]{1,0:T(8,128)} async-done(((f32[4608,512]{1,0:T(8,128)}), f32[1152,512]{1,0:T(8,128)}) %reduce-scatter.49.cloned.1.call-update) | async-done | bytes 2359312 | tf_op jit(solution)/shard_map/reduce_scatter | solution.py:190
  1506.6 94.9 %reduce-scatter.51.cloned.1.call-done = f32[1152,512]{1,0:T(8,128)} async-done(((f32[4608,512]{1,0:T(8,128)}), f32[1152,512]{1,0:T(8,128)}) %reduce-scatter.51.cloned.1.call-update) | async-done | bytes 2359312 | tf_op jit(solution)/shard_map/reduce_scatter | solution.py:190
  1606.0 24.8 %reduce-scatter.77.cloned.1.call-done = f32[32,128]{1,0:T(8,128)} async-done(((f32[256,128]{1,0:T(8,128)}), f32[32,128]{1,0:T(8,128)}) %reduce-scatter.77.cloned.1.call-update) | async-done | bytes 16400
  1631.7 30.2 %reduce-scatter.79.cloned.1.call-done = f32[32,128]{1,0:T(8,128)} async-done(((f32[256,128]{1,0:T(8,128)}), f32[32,128]{1,0:T(8,128)}) %reduce-scatter.79.cloned.1.call-update) | async-done | bytes 16400
  1663.4 30.3 %reduce-scatter.43.cloned.1.call-done = f32[192,64]{0,1:T(8,128)} async-done(((f32[192,512]{0,1:T(8,128)}), f32[192,64]{0,1:T(8,128)}) %reduce-scatter.43.cloned.1.call-update) | async-done | bytes 49168 | tf_op jit(solution)/shard_map/reduce_scatter | solution.py:191
  1693.7 31.9 %reduce-scatter.41.cloned.1.call-done = f32[192,64]{0,1:T(8,128)} async-done(((f32[192,512]{0,1:T(8,128)}), f32[192,64]{0,1:T(8,128)}) %reduce-scatter.41.cloned.1.call-update) | async-done | bytes 49168 | tf_op jit(solution)/shard_map/reduce_scatter | solution.py:191
  1727.1 288.4 %all-reduce.41.cloned.1.call-done = (f32[16384]{0:T(1024)}, f32[16384,256]{1,0:T(8,128)}) async-done(((f32[16384]{0:T(1024)}, f32[16384,256]{1,0:T(8,128)}), (f32[16384]{0:T(1024)}, f32[16384,256]{1,0:T(8,128)})) %all-reduce.41.cloned.1.call-update) | async-done | bytes 16842768 | tf_op jit(solution)/shard_map/psum | solution.py:389
  2018.5 28.5 %reduce-scatter.75.cloned.1.call-done = f32[64,512]{1,0:T(8,128)} async-done(((f32[512,512]{1,0:T(8,128)}), f32[64,512]{1,0:T(8,128)}) %reduce-scatter.75.cloned.1.call-update) | async-done | bytes 131088
  2047.0 33.5 %reduce-scatter.73.cloned.1.call-done = f32[64,512]{1,0:T(8,128)} async-done(((f32[512,512]{1,0:T(8,128)}), f32[64,512]{1,0:T(8,128)}) %reduce-scatter.73.cloned.1.call-update) | async-done | bytes 131088
  2082.2 35.2 %reduce-scatter.65.cloned.1.call-done = f32[64,1152]{1,0:T(8,128)} async-done(((f32[512,1152]{1,0:T(8,128)}), f32[64,1152]{1,0:T(8,128)}) %reduce-scatter.65.cloned.1.call-update) | async-done | bytes 294928
  2117.4 37.8 %reduce-scatter.67.cloned.1.call-done = f32[64,1152]{1,0:T(8,128)} async-done(((f32[512,1152]{1,0:T(8,128)}), f32[64,1152]{1,0:T(8,128)}) %reduce-scatter.67.cloned.1.call-update) | async-done | bytes 294928
  2155.2 37.6 %reduce-scatter.69.cloned.1.call-done = f32[64,1152]{1,0:T(8,128)} async-done(((f32[512,1152]{1,0:T(8,128)}), f32[64,1152]{1,0:T(8,128)}) %reduce-scatter.69.cloned.1.call-update) | async-done | bytes 294928
  2192.9 37.8 %reduce-scatter.71.cloned.1.call-done = f32[64,1152]{1,0:T(8,128)} async-done(((f32[512,1152]{1,0:T(8,128)}), f32[64,1152]{1,0:T(8,128)}) %reduce-scatter.71.cloned.1.call-update) | async-done | bytes 294928
  2235.6 44.7 %all-reduce.37 = (f32[1]{0:T(128)}, f32[1]{0:T(128)}, f32[]{:T(128)}, f32[8,512]{1,0:T(8,128)}) all-reduce(f32[1]{0:T(128)} %bitcast.148, f32[1]{0:T(128)} %bitcast.146, f32[]{:T(128)S(6)} %add.1566, f32[8,512]{1,0:T(8,128)} %stack.107), channel_id=1, replica_groups=mesh['dp'=8,'fsdp'=4] {'dp','fsdp'}, use_global_device_ids=true, to_apply=%region_29.32 | all-reduce | flops 4099 | bytes 32792 | tf_op jit(solution)/shard_map/psum | solution.py:353
  (1197 shorter events, 1022.0 us)
Async XLA Ops:
  7.2 311.8 %all-gather.15.cloned.1.call-start = ((), (), s32[]{:S(2)}) async-start(), calls=%async_computation.34 | async-start | bytes 1327104 | tf_op jit(solution)/shard_map/all_gather | solution.py:150
  9.5 314.9 %all-gather.17.cloned.1.call-start = ((), (), s32[]{:S(2)}) async-start(), calls=%async_computation.35 | async-start | bytes 1327104 | tf_op jit(solution)/shard_map/all_gather | solution.py:150
  10.2 319.4 %all-gather.19.cloned.1.call-start = ((), (), s32[]{:S(2)}) async-start(), calls=%async_computation.36 | async-start | bytes 1327104 | tf_op jit(solution)/shard_map/all_gather | solution.py:150
  24.5 176.3 %collective-permute-start.12 = (bf16[128,256]{0,1:T(8,128)(2,1)S(1)}, bf16[128,256]{0,1:T(8,128)(2,1)}, u32[]{:S(2)}, u32[]{:S(2)}) collective-permute-start(bf16[128,256]{0,1:T(8,128)(2,1)S(1)} %bitcast.1048), channel_id=1, source_target_pairs={{0,1},{1,2},{2,3},{3,0},{4,5},{5,6},{6,7},{7,4},{8,9},{9,10},{10,1... | collective-permute-start | bytes 196616 | tf_op jit(solution)/shard_map/ppermute | solution.py:162
  26.0 179.6 %collective-permute-start.13 = (bf16[128,256]{0,1:T(8,128)(2,1)S(1)}, bf16[128,256]{0,1:T(8,128)(2,1)}, u32[]{:S(2)}, u32[]{:S(2)}) collective-permute-start(bf16[128,256]{0,1:T(8,128)(2,1)S(1)} %bitcast.1049), channel_id=1, source_target_pairs={{0,3},{1,0},{2,1},{3,2},{4,7},{5,4},{6,5},{7,6},{8,11},{9,8},{10,9... | collective-permute-start | bytes 196616 | tf_op jit(solution)/shard_map/ppermute | solution.py:171
  98.5 257.3 %all-gather.21.cloned.1.call-start = ((), (), s32[]{:S(2)}) async-start(), calls=%async_computation.37 | async-start | bytes 1327104 | tf_op jit(solution)/shard_map/all_gather | solution.py:150
  319.1 823.3 %reduce-scatter.57.cloned.1.call-start = ((), (), s32[]{:S(2)}) async-start(), calls=%async_computation.32 | async-start | bytes 655360 | tf_op jit(solution)/shard_map/reduce_scatter | solution.py:190
  510.6 238.6 %collective-permute-start.26 = (bf16[1152,512]{1,0:T(8,128)(2,1)}, bf16[1152,512]{1,0:T(8,128)(2,1)}, u32[]{:S(2)}, u32[]{:S(2)}) collective-permute-start(bf16[1152,512]{1,0:T(8,128)(2,1)} %collective-permute-done.24), channel_id=1, source_target_pairs={{0,1},{1,2},{2,3},{3,0},{4,5},{5,6},{6,7},{7,4},{8,9},{9,10},{10,1... | collective-permute-start | bytes 3538952 | tf_op jit(solution)/shard_map/ppermute | solution.py:162
  962.7 181.5 %reduce-scatter.59.cloned.1.call-start = ((), (), s32[]{:S(2)}) async-start(), calls=%async_computation.33 | async-start | bytes 655360 | tf_op jit(solution)/shard_map/reduce_scatter | solution.py:190
  1069.2 238.1 %reduce-scatter.45.cloned.1.call-start = ((), (), s32[]{:S(2)}) async-start(), calls=%async_computation.26 | async-start | bytes 11796480 | tf_op jit(solution)/shard_map/reduce_scatter | solution.py:190
  1085.8 319.4 %reduce-scatter.47.cloned.1.call-start = ((), (), s32[]{:S(2)}) async-start(), calls=%async_computation.27 | async-start | bytes 11796480 | tf_op jit(solution)/shard_map/reduce_scatter | solution.py:190
  1103.1 400.4 %reduce-scatter.49.cloned.1.call-start = ((), (), s32[]{:S(2)}) async-start(), calls=%async_computation.28 | async-start | bytes 11796480 | tf_op jit(solution)/shard_map/reduce_scatter | solution.py:190
  1125.0 476.5 %reduce-scatter.51.cloned.1.call-start = ((), (), s32[]{:S(2)}) async-start(), calls=%async_computation.29 | async-start | bytes 11796480 | tf_op jit(solution)/shard_map/reduce_scatter | solution.py:190
  1142.3 488.5 %reduce-scatter.77.cloned.1.call-start = ((), (), s32[]{:S(2)}) async-start(), calls=%async_computation.46 | async-start | bytes 147456
  1144.1 517.8 %reduce-scatter.79.cloned.1.call-start = ((), (), s32[]{:S(2)}) async-start(), calls=%async_computation.47 | async-start | bytes 147456
  1145.9 547.8 %reduce-scatter.43.cloned.1.call-start = ((), (), s32[]{:S(2)}) async-start(), calls=%async_computation.25 | async-start | bytes 589824 | tf_op jit(solution)/shard_map/reduce_scatter | solution.py:191
  1148.0 577.6 %reduce-scatter.41.cloned.1.call-start = ((), (), s32[]{:S(2)}) async-start(), calls=%async_computation.24 | async-start | bytes 589824 | tf_op jit(solution)/shard_map/reduce_scatter | solution.py:191
  1150.1 865.4 %all-reduce.41.cloned.1.call-start = ((), (), s32[]{:S(2)}) async-start(), calls=%async_computation.48 | async-start | bytes 33685504 | tf_op jit(solution)/shard_map/psum | solution.py:389
  1200.4 846.6 %reduce-scatter.75.cloned.1.call-start = ((), (), s32[]{:S(2)}) async-start(), calls=%async_computation.45 | async-start | bytes 1179648
  1203.0 877.5 %reduce-scatter.73.cloned.1.call-start = ((), (), s32[]{:S(2)}) async-start(), calls=%async_computation.44 | async-start | bytes 1179648
  1211.7 905.8 %reduce-scatter.65.cloned.1.call-start = ((), (), s32[]{:S(2)}) async-start(), calls=%async_computation.40 | async-start | bytes 2654208
  1310.4 844.9 %reduce-scatter.67.cloned.1.call-start = ((), (), s32[]{:S(2)}) async-start(), calls=%async_computation.41 | async-start | bytes 2654208
  1408.4 784.5 %reduce-scatter.69.cloned.1.call-start = ((), (), s32[]{:S(2)}) async-start(), calls=%async_computation.42 | async-start | bytes 2654208
  1506.6 724.1 %reduce-scatter.71.cloned.1.call-start = ((), (), s32[]{:S(2)}) async-start(), calls=%async_computation.43 | async-start | bytes 2654208
  (279 other events, 6532.6 us)
Sparse Core Ops, SparseCore 0:
  10.3 23.7 all-gather.14
  61.0 23.1 all-gather.18
  113.9 25.9 all-gather.20
  962.9 23.7 reduce-scatter.56
  1005.9 23.8 reduce-scatter.58
  1032.8 30.8 reduce-scatter.62
  1066.7 30.9 reduce-scatter.60
  1100.6 52.6 reduce-scatter.54
  1156.4 52.6 reduce-scatter.52
  1212.2 94.9 reduce-scatter.44
  1310.2 95.0 reduce-scatter.46
  1408.4 95.0 reduce-scatter.48
  1506.4 95.0 reduce-scatter.50
  1604.2 26.6 reduce-scatter.76
  1633.6 28.2 reduce-scatter.78
  1664.6 29.0 reduce-scatter.42
  1696.5 29.1 reduce-scatter.40
  1732.6 282.8 all-reduce.40
  2018.3 28.7 reduce-scatter.74
  2049.9 30.6 reduce-scatter.72
  2082.9 34.4 reduce-scatter.64
  2119.8 35.4 reduce-scatter.66
  2157.4 35.4 reduce-scatter.68
  2195.2 35.4 reduce-scatter.70
  (1 shorter events, 22.4 us)
